TPU v7x, 32 devices: a whole 2x2x4 slice. The times are simulated.
32 devices in a mesh: blk: 8 (over y, x, core), feat: 4 (over z).
Axes of the slice: x: 2, y: 2, z: 4, core: 2. Of those that a mesh axis runs over, the one named last changes fastest.
Arguments:
- node_feats: bfloat16 [8192, 512], P('blk', 'feat'), may hold values from -6 to 6
- weight: bfloat16 [512, 512], P(None, 'feat'), may hold values from -0.25 to 0.25
- tile_value: bfloat16 [8, 5, 8, 128, 128], P('blk'), may hold values from -0.75 to 0.75
- tile_row: int32 [8, 5, 8], P('blk'), may hold values from 0 to 7
- tile_col: int32 [8, 5, 8], P('blk'), may hold values from 0 to 7
- tile_count: int32 [8, 5], P('blk'), may hold values from 2 to 8, as said below
- grad_out: bfloat16 [8192, 512], P('blk', 'feat'), may hold values from -6 to 6
Outputs:
- output_y: bfloat16 [8192, 512], P('blk', 'feat')
- grad_x: bfloat16 [8192, 512], P('blk', 'feat')
- grad_w: float32 [512, 512], P(None, 'feat')
Inputs may be any that keep to these rules, and one draw needn't show every extreme that they name: `tile_count`: in every draw one owner has all 8 slots live for every distance; owners differ in how many tiles they hold.
All inputs are finite; a program needn't handle non-finite values.
Results may differ from a plain program's by a relative error of at most 0.0062.
Values may be sent and summed in bfloat16 or wider, within the bound.
A program may use at most 64 MiB of HBM per device.

v0:
```python
import jax
import jax.numpy as jnp
from jax import lax
from jax.sharding import PartitionSpec as P


def shifted(block, axis, distance):
    devices = range(lax.axis_size(axis))
    route = [((i - distance) % len(devices), i) for i in devices]
    return lax.ppermute(block, axis, route)


def on_device(node_feats, weight, tile_value, tile_row, tile_col, tile_count, grad_out):
    tile_side = tile_value.shape[-1]
    blocks = node_feats.shape[0] // tile_side
    feat_width = weight.shape[1]
    offsets = tile_value.shape[1]
    reach_count = (offsets - 1) // 2
    slot_ids = jnp.arange(tile_value.shape[2], dtype=jnp.int32)
    block_ids = jnp.arange(blocks, dtype=jnp.int32)
    live_slots = slot_ids[None, :] < tile_count[0][:, None]
    row_onehot = (
        (tile_row[0][:, None, :] == block_ids[None, :, None]) & live_slots[:, None, :]
    ).astype(jnp.float32)
    col_onehot = (
        (tile_col[0][:, None, :] == block_ids[None, :, None]) & live_slots[:, None, :]
    ).astype(jnp.float32)
    full_feats = lax.all_gather(node_feats, "feat", axis=1, tiled=True)
    hidden = jnp.dot(full_feats, weight, preferred_element_type=jnp.float32).astype(jnp.bfloat16)
    panel_own = hidden.reshape(blocks, tile_side, feat_width)
    wanted_lists = {}
    picked = jnp.take(panel_own, tile_col[0, reach_count], axis=0)
    gather_product = jnp.einsum(
        "sij,sjf->sif", tile_value[0, reach_count], picked, preferred_element_type=jnp.float32
    )
    aggregate = jnp.einsum(
        "rs,sif->rif", row_onehot[reach_count], gather_product, precision=lax.Precision.HIGHEST
    )
    for distance in range(-reach_count, reach_count + 1):
        if distance != 0:
            offset = distance + reach_count
            wanted = shifted(tile_col[0, offset], "blk", distance)
            wanted_lists[distance] = wanted
            sent_blocks = jnp.take(panel_own, wanted, axis=0)
            arrived = shifted(sent_blocks, "blk", -distance)
            product = jnp.einsum(
                "sij,sjf->sif", tile_value[0, offset], arrived, preferred_element_type=jnp.float32
            )
            aggregate = aggregate + jnp.einsum(
                "rs,sif->rif", row_onehot[offset], product, precision=lax.Precision.HIGHEST
            )
    preact = aggregate.reshape(blocks * tile_side, feat_width) + hidden.astype(jnp.float32)
    output_y = jax.nn.silu(preact).astype(jnp.bfloat16)
    sigmoid_pre = jax.nn.sigmoid(preact)
    slope_term = sigmoid_pre * (1.0 + preact * (1.0 - sigmoid_pre))
    grad_pre = (grad_out.astype(jnp.float32) * slope_term).astype(jnp.bfloat16)
    grad_blocks = grad_pre.reshape(blocks, tile_side, feat_width)

    def slot_products(offset):
        picked = jnp.take(grad_blocks, tile_row[0, offset], axis=0)
        return jnp.einsum(
            "sji,sjf->sif", tile_value[0, offset], picked, preferred_element_type=jnp.float32
        )

    transposed = jnp.einsum(
        "cs,sif->cif",
        col_onehot[reach_count],
        slot_products(reach_count),
        precision=lax.Precision.HIGHEST,
    )
    for distance in range(-reach_count, reach_count + 1):
        if distance != 0:
            offset = distance + reach_count
            masked = slot_products(offset) * live_slots[offset][:, None, None].astype(jnp.float32)
            received = shifted(masked, "blk", distance)
            target_onehot = (wanted_lists[distance][None, :] == block_ids[:, None]).astype(
                jnp.float32
            )
            transposed = transposed + jnp.einsum(
                "cs,sif->cif", target_onehot, received, precision=lax.Precision.HIGHEST
            )
    grad_hidden = (
        grad_pre.astype(jnp.float32) + transposed.reshape(blocks * tile_side, feat_width)
    ).astype(jnp.bfloat16)
    weight_term = lax.dot_general(
        full_feats, grad_hidden, (((0,), (0,)), ((), ())), preferred_element_type=jnp.float32
    )
    grad_w = lax.psum(weight_term, "blk")
    partial_grad = lax.dot_general(
        grad_hidden, weight, (((1,), (1,)), ((), ())), preferred_element_type=jnp.float32
    )
    grad_x = lax.psum_scatter(partial_grad, "feat", scatter_dimension=1, tiled=True).astype(
        jnp.bfloat16
    )
    return (output_y, grad_x, grad_w)


def solution(mesh):
    return jax.shard_map(
        on_device,
        mesh=mesh,
        in_specs=(
            P("blk", "feat"),
            P(None, "feat"),
            P("blk", None, None, None, None),
            P("blk", None, None),
            P("blk", None, None),
            P("blk", None),
            P("blk", "feat"),
        ),
        out_specs=(P("blk", "feat"), P("blk", "feat"), P(None, "feat")),
        check_vma=False,
    )
```

profile of v0, /device:TPU:0, one launch (start us, length us, event | category | flops | bytes accessed | tf_op | source)
XLA Modules:
  0.0 216.4 jit_solution(13034620834880448403)
XLA Ops:
  8.7 3.9 %collective-permute-start = (s32[8]{0:T(128)S(1)}, s32[8]{0:T(128)S(1)}, u32[]{:S(2)}, u32[]{:S(2)}) collective-permute-start(s32[8]{0:T(128)S(1)} %get-tuple-element.32), channel_id=1, source_target_pairs={{8,0},{12,4},{16,8},{20,12},{24,16},{28,20},{0,24},{4,28},{9,1},{1... | collective-permute-start | bytes 104 | tf_op jit(solution)/shard_map/ppermute | solution.py:10
  15.1 1.3 compare_and_fusion.2
  22.6 19.6 %all-gather.2.cloned.1.call-done = bf16[1024,512]{1,0:T(8,128)(2,1)} async-done(((bf16[1024,128]{1,0:T(8,128)(2,1)}), bf16[1024,512]{1,0:T(8,128)(2,1)}) %all-gather.2.cloned.1.call-update) | async-done | bytes 1048592 | tf_op jit(solution)/shard_map/all_gather | solution.py:28
  42.2 1.7 convolution_convert_fusion
  49.6 2.6 %collective-permute-start.5 = (bf16[8,128,128]{2,1,0:T(8,128)(2,1)}, bf16[8,128,128]{2,1,0:T(8,128)(2,1)}, u32[]{:S(2)}, u32[]{:S(2)}) collective-permute-start(bf16[8,128,128]{2,1,0:T(8,128)(2,1)} %broadcast_select_fusion.1), channel_id=1, source_target_pairs={{4,0},{8,4},{12,8},{16,12},{20,16},{24,20},{28,24},{0,28},{5,1},{9... | collective-permute-start | bytes 786440 | tf_op jit(solution)/shard_map/ppermute | solution.py:10
  53.7 1.3 collective-permute-start.7
  55.4 1.3 fusion.25
  56.7 1.3 fusion.21
  58.0 1.0 copy.14
  59.0 1.0 copy.15
  60.0 1.3 fusion.17
  61.3 1.0 copy.16
  62.3 1.8 collective-permute-done.7
  64.4 1.0 copy.17
  68.5 1.0 multiply_convert_fusion
  71.0 0.9 multiply_bitcast_fusion.3
  71.9 1.5 collective-permute-start.8
  75.3 0.9 multiply_bitcast_fusion.1
  81.3 2.4 %collective-permute-start.9 = (f32[8,128,128]{2,0,1:T(8,128)S(1)}, f32[8,128,128]{2,0,1:T(8,128)S(1)}, u32[]{:S(2)}, u32[]{:S(2)}) collective-permute-start(f32[8,128,128]{2,0,1:T(8,128)S(1)} %multiply_bitcast_fusion.2), channel_id=1, source_target_pairs={{4,0},{8,4},{12,8},{16,12},{20,16},{24,20},{28,24},{0,28},{5,1},{9... | collective-permute-start | bytes 1572872 | tf_op jit(solution)/shard_map/ppermute | solution.py:10
  84.1 9.4 %collective-permute-done.10 = f32[8,128,128]{2,0,1:T(8,128)} collective-permute-done((f32[8,128,128]{2,0,1:T(8,128)}, f32[8,128,128]{2,0,1:T(8,128)}, u32[]{:S(2)}, u32[]{:S(2)}) %collective-permute-start.10) | collective-permute-done | bytes 524320 | tf_op jit(solution)/shard_map/ppermute | solution.py:10
  93.4 1.4 fusion.65
  94.8 3.1 %collective-permute-done.11 = f32[8,128,128]{2,0,1:T(8,128)} collective-permute-done((f32[8,128,128]{2,0,1:T(8,128)}, f32[8,128,128]{2,0,1:T(8,128)}, u32[]{:S(2)}, u32[]{:S(2)}) %collective-permute-start.11) | collective-permute-done | bytes 524320 | tf_op jit(solution)/shard_map/ppermute | solution.py:10
  97.9 1.4 fusion.68
  99.4 1.4 convolution_add_fusion.1
  100.8 5.3 %collective-permute-done.9 = f32[8,128,128]{2,0,1:T(8,128)S(1)} collective-permute-done((f32[8,128,128]{2,0,1:T(8,128)S(1)}, f32[8,128,128]{2,0,1:T(8,128)S(1)}, u32[]{:S(2)}, u32[]{:S(2)}) %collective-permute-start.9) | collective-permute-done | bytes 524320 | tf_op jit(solution)/shard_map/ppermute | solution.py:10
  106.7 1.0 copy-done.2
  107.7 1.0 convolution_bitcast_fusion
  108.8 1.8 fusion.89
  110.6 52.1 %all-reduce.2.cloned.1.call-done = f32[512,128]{0,1:T(8,128)} async-done(((f32[512,128]{0,1:T(8,128)}), f32[512,128]{0,1:T(8,128)}) %all-reduce.2.cloned.1.call-update) | async-done | bytes 262160 | tf_op jit(solution)/shard_map/psum | solution.py:88
  162.7 1.8 copy.12
  164.5 43.6 %reduce-scatter.2.cloned.1.call-done = f32[1024,128]{1,0:T(8,128)} async-done(((f32[1024,512]{1,0:T(8,128)}), f32[1024,128]{1,0:T(8,128)}) %reduce-scatter.2.cloned.1.call-update) | async-done | bytes 524304 | tf_op jit(solution)/shard_map/reduce_scatter | solution.py:92
  208.1 1.8 convert_element_type.89
  (141 shorter events, 30.1 us)
Async XLA Ops:
  7.2 35.1 %copy-start = (bf16[512,128]{1,0:T(8,128)(2,1)S(1)}, bf16[512,128]{1,0:T(8,128)(2,1)}, u32[]{:S(2)}) copy-start(bf16[512,128]{1,0:T(8,128)(2,1)} %param.10) | copy-start | bytes 393220
  7.2 35.1 %all-gather.2.cloned.1.call-start = ((), (), s32[]{:S(2)}) async-start(), calls=%async_computation.1 | async-start | bytes 1310720 | tf_op jit(solution)/shard_map/all_gather | solution.py:28
  7.9 154.8 %all-reduce.2.cloned.1.call-start = ((), (), s32[]{:S(2)}) async-start(), calls=%async_computation.3 | async-start | bytes 524288 | tf_op jit(solution)/shard_map/psum | solution.py:88
  8.7 11.6 %collective-permute-start = (s32[8]{0:T(128)S(1)}, s32[8]{0:T(128)S(1)}, u32[]{:S(2)}, u32[]{:S(2)}) collective-permute-start(s32[8]{0:T(128)S(1)} %get-tuple-element.32), channel_id=1, source_target_pairs={{8,0},{12,4},{16,8},{20,12},{24,16},{28,20},{0,24},{4,28},{9,1},{1... | collective-permute-start | bytes 104 | tf_op jit(solution)/shard_map/ppermute | solution.py:10
  12.6 7.7 %collective-permute-start.2 = (s32[8]{0:T(128)S(1)}, s32[8]{0:T(128)S(1)}, u32[]{:S(2)}, u32[]{:S(2)}) collective-permute-start(s32[8]{0:T(128)S(1)} %get-tuple-element.31), channel_id=1, source_target_pairs={{4,0},{8,4},{12,8},{16,12},{20,16},{24,20},{28,24},{0,28},{5,1},{9... | collective-permute-start | bytes 104 | tf_op jit(solution)/shard_map/ppermute | solution.py:10
  12.6 7.7 %collective-permute-start.4 = (s32[8]{0:T(128)S(1)}, s32[8]{0:T(128)S(1)}, u32[]{:S(2)}, u32[]{:S(2)}) collective-permute-start(s32[8]{0:T(128)S(1)} %get-tuple-element.30), channel_id=1, source_target_pairs={{28,0},{0,4},{4,8},{8,12},{12,16},{16,20},{20,24},{24,28},{29,1},{... | collective-permute-start | bytes 104 | tf_op jit(solution)/shard_map/ppermute | solution.py:10
  13.1 7.8 %collective-permute-start.6 = (s32[8]{0:T(128)S(1)}, s32[8]{0:T(128)S(1)}, u32[]{:S(2)}, u32[]{:S(2)}) collective-permute-start(s32[8]{0:T(128)S(1)} %get-tuple-element.29), channel_id=1, source_target_pairs={{24,0},{28,4},{0,8},{4,12},{8,16},{12,20},{16,24},{20,28},{25,1},{... | collective-permute-start | bytes 104 | tf_op jit(solution)/shard_map/ppermute | solution.py:10
  20.2 25.7 %copy-start.19 = (s32[8]{0:T(128)}, s32[8]{0:T(128)S(1)}, u32[]{:S(2)}) copy-start(s32[8]{0:T(128)S(1)} %collective-permute-done) | copy-start | bytes 100
  20.3 25.7 %copy-start.27 = (s32[8]{0:T(128)}, s32[8]{0:T(128)S(1)}, u32[]{:S(2)}) copy-start(s32[8]{0:T(128)S(1)} %collective-permute-done.2) | copy-start | bytes 100
  20.3 25.7 %copy-start.23 = (s32[8]{0:T(128)}, s32[8]{0:T(128)S(1)}, u32[]{:S(2)}) copy-start(s32[8]{0:T(128)S(1)} %collective-permute-done.4) | copy-start | bytes 100
  20.9 25.0 %copy-start.21 = (s32[8]{0:T(128)}, s32[8]{0:T(128)S(1)}, u32[]{:S(2)}) copy-start(s32[8]{0:T(128)S(1)} %collective-permute-done.6) | copy-start | bytes 100
  22.6 23.4 %copy-start.1 = (bf16[1,5,8,128,128]{4,3,2,1,0:T(8,128)(2,1)S(1)}, bf16[1,5,8,128,128]{4,3,2,1,0:T(8,128)(2,1)}, u32[]{:S(2)}) copy-start(bf16[1,5,8,128,128]{4,3,2,1,0:T(8,128)(2,1)} %param.11) | copy-start | bytes 3932164
  44.6 10.8 %collective-permute-start.1 = (bf16[8,128,128]{2,1,0:T(8,128)(2,1)S(1)}, bf16[8,128,128]{2,1,0:T(8,128)(2,1)}, u32[]{:S(2)}, u32[]{:S(2)}) collective-permute-start(bf16[8,128,128]{2,1,0:T(8,128)(2,1)S(1)} %broadcast_select_fusion.3), channel_id=1, source_target_pairs={{24,0},{28,4},{0,8},{4,12},{8,16},{12,20},{16,24},{20,28},{25,1},{... | collective-permute-start | bytes 786440 | tf_op jit(solution)/shard_map/ppermute | solution.py:10
  46.7 6.2 %copy-start.25 = (pred[8]{0:T(512)(128)(4,1)S(1)}, pred[8]{0:T(512)(128)(4,1)}, u32[]{:S(2)}) copy-start(pred[8]{0:T(512)(128)(4,1)} %compare_and_fusion.5) | copy-start | bytes 28
  48.0 8.6 %collective-permute-start.3 = (bf16[8,128,128]{2,1,0:T(8,128)(2,1)S(1)}, bf16[8,128,128]{2,1,0:T(8,128)(2,1)}, u32[]{:S(2)}, u32[]{:S(2)}) collective-permute-start(bf16[8,128,128]{2,1,0:T(8,128)(2,1)S(1)} %broadcast_select_fusion.2), channel_id=1, source_target_pairs={{28,0},{0,4},{4,8},{8,12},{12,16},{16,20},{20,24},{24,28},{29,1},{... | collective-permute-start | bytes 786440 | tf_op jit(solution)/shard_map/ppermute | solution.py:10
  49.6 10.4 %collective-permute-start.5 = (bf16[8,128,128]{2,1,0:T(8,128)(2,1)}, bf16[8,128,128]{2,1,0:T(8,128)(2,1)}, u32[]{:S(2)}, u32[]{:S(2)}) collective-permute-start(bf16[8,128,128]{2,1,0:T(8,128)(2,1)} %broadcast_select_fusion.1), channel_id=1, source_target_pairs={{4,0},{8,4},{12,8},{16,12},{20,16},{24,20},{28,24},{0,28},{5,1},{9... | collective-permute-start | bytes 786440 | tf_op jit(solution)/shard_map/ppermute | solution.py:10
  53.7 10.4 %collective-permute-start.7 = (bf16[8,128,128]{2,1,0:T(8,128)(2,1)}, bf16[8,128,128]{2,1,0:T(8,128)(2,1)S(1)}, u32[]{:S(2)}, u32[]{:S(2)}) collective-permute-start(bf16[8,128,128]{2,1,0:T(8,128)(2,1)} %broadcast_select_fusion), channel_id=1, source_target_pairs={{8,0},{12,4},{16,8},{20,12},{24,16},{28,20},{0,24},{4,28},{9,1},{1... | collective-permute-start | bytes 786440 | tf_op jit(solution)/shard_map/ppermute | solution.py:10
  62.3 3.1 %copy-start.3 = (f32[8,128,128]{1,0,2:T(8,128)S(1)}, f32[8,128,128]{1,0,2:T(8,128)}, u32[]{:S(2)}) copy-start(f32[8,128,128]{1,0,2:T(8,128)} %copy.14) | copy-start | bytes 1572868
  70.9 3.7 %copy-start.16 = (pred[8]{0:T(512)(128)(4,1)S(1)}, pred[8]{0:T(512)(128)(4,1)}, u32[]{:S(2)}) copy-start(pred[8]{0:T(512)(128)(4,1)} %get-tuple-element.27) | copy-start | bytes 28
  71.9 27.5 %collective-permute-start.8 = (f32[8,128,128]{2,0,1:T(8,128)}, f32[8,128,128]{2,0,1:T(8,128)}, u32[]{:S(2)}, u32[]{:S(2)}) collective-permute-start(f32[8,128,128]{2,0,1:T(8,128)} %multiply_bitcast_fusion.3), channel_id=1, source_target_pairs={{8,0},{12,4},{16,8},{20,12},{24,16},{28,20},{0,24},{4,28},{9,1},{1... | collective-permute-start | bytes 1572872 | tf_op jit(solution)/shard_map/ppermute | solution.py:10
  76.2 17.2 %collective-permute-start.10 = (f32[8,128,128]{2,0,1:T(8,128)}, f32[8,128,128]{2,0,1:T(8,128)}, u32[]{:S(2)}, u32[]{:S(2)}) collective-permute-start(f32[8,128,128]{2,0,1:T(8,128)} %multiply_bitcast_fusion.1), channel_id=1, source_target_pairs={{28,0},{0,4},{4,8},{8,12},{12,16},{16,20},{20,24},{24,28},{29,1},{... | collective-permute-start | bytes 1572872 | tf_op jit(solution)/shard_map/ppermute | solution.py:10
  77.4 2.5 %copy-start.14 = (pred[8]{0:T(512)(128)(4,1)S(1)}, pred[8]{0:T(512)(128)(4,1)}, u32[]{:S(2)}) copy-start(pred[8]{0:T(512)(128)(4,1)} %get-tuple-element.23) | copy-start | bytes 28
  77.7 2.6 %copy-start.13 = (pred[8]{0:T(512)(128)(4,1)S(1)}, pred[8]{0:T(512)(128)(4,1)}, u32[]{:S(2)}) copy-start(pred[8]{0:T(512)(128)(4,1)} %get-tuple-element.7) | copy-start | bytes 28
  78.6 19.4 %collective-permute-start.11 = (f32[8,128,128]{2,0,1:T(8,128)}, f32[8,128,128]{2,0,1:T(8,128)}, u32[]{:S(2)}, u32[]{:S(2)}) collective-permute-start(f32[8,128,128]{2,0,1:T(8,128)} %multiply_bitcast_fusion), channel_id=1, source_target_pairs={{24,0},{28,4},{0,8},{4,12},{8,16},{12,20},{16,24},{20,28},{25,1},{... | collective-permute-start | bytes 1572872 | tf_op jit(solution)/shard_map/ppermute | solution.py:10
  80.8 2.8 %copy-start.8 = (pred[1,8]{1,0:T(4,128)(4,1)S(1)}, pred[1,8]{1,0:T(4,128)(4,1)}, u32[]{:S(2)}) copy-start(pred[1,8]{1,0:T(4,128)(4,1)} %get-tuple-element.34) | copy-start | bytes 28
  80.8 2.8 %copy-start.18 = (s32[1,8]{1,0:T(1,128)S(1)}, s32[1,8]{1,0:T(1,128)}, u32[]{:S(2)}) copy-start(s32[1,8]{1,0:T(1,128)} %slice.130) | copy-start | bytes 100
  81.0 12.4 %copy-start.24 = (s32[8]{0:T(128)S(1)}, s32[8]{0:T(128)}, u32[]{:S(2)}) copy-start(s32[8]{0:T(128)} %copy-done.23) | copy-start | bytes 100
  81.3 16.7 %copy-start.22 = (s32[8]{0:T(128)S(1)}, s32[8]{0:T(128)}, u32[]{:S(2)}) copy-start(s32[8]{0:T(128)} %copy-done.21) | copy-start | bytes 100
  81.3 24.8 %collective-permute-start.9 = (f32[8,128,128]{2,0,1:T(8,128)S(1)}, f32[8,128,128]{2,0,1:T(8,128)S(1)}, u32[]{:S(2)}, u32[]{:S(2)}) collective-permute-start(f32[8,128,128]{2,0,1:T(8,128)S(1)} %multiply_bitcast_fusion.2), channel_id=1, source_target_pairs={{4,0},{8,4},{12,8},{16,12},{20,16},{24,20},{28,24},{0,28},{5,1},{9... | collective-permute-start | bytes 1572872 | tf_op jit(solution)/shard_map/ppermute | solution.py:10
  84.1 15.3 %copy-start.20 = (s32[8]{0:T(128)S(1)}, s32[8]{0:T(128)}, u32[]{:S(2)}) copy-start(s32[8]{0:T(128)} %copy-done.19) | copy-start | bytes 100
  94.8 11.2 %copy-start.28 = (s32[8]{0:T(128)S(1)}, s32[8]{0:T(128)}, u32[]{:S(2)}) copy-start(s32[8]{0:T(128)} %copy-done.27) | copy-start | bytes 100
  108.8 99.3 %reduce-scatter.2.cloned.1.call-start = ((), (), s32[]{:S(2)}) async-start(), calls=%async_computation.2 | async-start | bytes 2621440 | tf_op jit(solution)/shard_map/reduce_scatter | solution.py:92
  (12 other events, 16.7 us)
Sparse Core Ops, SparseCore 0:
  9.5 32.6 all-gather.1
  108.9 53.7 all-reduce.1
  165.0 43.0 reduce-scatter.1
where the time goes:
time: 217 us; the launch traced here: 216 us
  waiting for transfers between devices  136 us (63%)
  local copies, waits for them, and re-layouts  19.5 us (9%)
  matrix products  17.6 us (8%)
  other arithmetic  14.8 us (7%)
  starting transfers between devices  14.4 us (7%)
  between operations  14.4 us (7%)
    psum x1, waiting for transfers between devices, on_device(): grad_w = lax.psum(weight_term, 'blk')  52.1 us
    reduce_scatter x1, waiting for transfers between devices, on_device(): lax.psum_scatter(partial_grad, 'feat', scatter_dimension=1, tiled=True)  43.6 us
    all_gather x1, waiting for transfers between devices, on_device(): full_feats = lax.all_gather(node_feats, 'feat', axis=1, tiled=True)  19.6 us
    ppermute x12, waiting for transfers between devices, shifted(): return lax.ppermute(block, axis, route)  19.6 us
    ppermute x12, starting transfers between devices, shifted(): return lax.ppermute(block, axis, route)  14.3 us
    unnamed x61, local copies, waits for them, and re-layouts  5.8 us
    dot_general x4, matrix products, on_device(): jnp.einsum('cs,sif->cif', target_onehot, received, precision=lax.Precisio...  4.6 us
  transfers between devices with their start and end apart: 15, of which 7 were waited for; matrix products, arithmetic and copies ran while one was open for 17% of the time, Pallas kernels for 0%

commit v1 on v0

--- a/solution.py
+++ b/solution.py
@@ -2,6 +2,28 @@
 import jax.numpy as jnp
 from jax import lax
 from jax.sharding import PartitionSpec as P
+
+
+def laid_out(blocks, dim):
+    shape = list(blocks.shape[1:])
+    shape[dim] *= blocks.shape[0]
+    return jnp.moveaxis(blocks, 0, dim).reshape(shape)
+
+
+def collected_by_bits(x, axis):
+    devices = lax.axis_size(axis)
+    tiles = x[None]
+    for level in range(devices.bit_length() - 1):
+        apart = 1 << level
+        other = lax.ppermute(tiles, axis, [(i, i ^ apart) for i in range(devices)])
+        both = jnp.stack([tiles, other])
+        upper = lax.axis_index(axis) >> level & 1
+        tiles = jnp.where(upper == 0, both, both[::-1]).reshape(-1, *x.shape)
+    return tiles
+
+
+def collect(shard, axis, dim):
+    return laid_out(collected_by_bits(shard, axis), dim)
 
 
 def shifted(block, axis, distance):
@@ -25,7 +47,7 @@
     col_onehot = (
         (tile_col[0][:, None, :] == block_ids[None, :, None]) & live_slots[:, None, :]
     ).astype(jnp.float32)
-    full_feats = lax.all_gather(node_feats, "feat", axis=1, tiled=True)
+    full_feats = collect(node_feats, "feat", 1)
     hidden = jnp.dot(full_feats, weight, preferred_element_type=jnp.float32).astype(jnp.bfloat16)
     panel_own = hidden.reshape(blocks, tile_side, feat_width)
     wanted_lists = {}

time: 217 us -> 194 us (0.89)
  waiting for transfers between devices: 136 us -> 84.8 us
  local copies, waits for them, and re-layouts: 19.5 us -> 26.9 us
  other arithmetic: 14.8 us -> 22 us
  matrix products: 17.6 us -> 24.5 us
  starting transfers between devices: 14.4 us -> 18.6 us
    psum x1, waiting for transfers between devices: 52.1 us -> 11.9 us  [on_device(): grad_w = lax.psum(weight_term, 'blk')]
    ppermute x0 -> x2, waiting for transfers between devices: none -> 22.5 us  [collected_by_bits(): other = lax.ppermute(tiles, axis, [(i, i ^ apart) for i in range(devices)])]
    all_gather x1 -> x0, waiting for transfers between devices: 19.6 us -> none  [on_device(): full_feats = lax.all_gather(node_feats, 'feat', axis=1, tiled=True)]
    ppermute x12, waiting for transfers between devices: 19.6 us -> 7.09 us  [shifted(): return lax.ppermute(block, axis, route)]
    ppermute x0 -> x2, starting transfers between devices: none -> 5.77 us  [collected_by_bits(): other = lax.ppermute(tiles, axis, [(i, i ^ apart) for i in range(devices)])]
    dot_general x5, matrix products: 1.74 us -> 5.41 us  [slot_products(): jnp.einsum('sji,sjf->sif', tile_value[0, offset], picked, preferred_eleme...]
    dot_general x5, local copies, waits for them, and re-layouts: 1.16 us -> 4.52 us  [slot_products(): jnp.einsum('sji,sjf->sif', tile_value[0, offset], picked, preferred_eleme...]
    mul x4, other arithmetic: 2.8 us -> 5.95 us  [on_device(): slot_products(offset)]
  transfers between devices with their start and end apart: 15 -> 16, of which waited for: 7 -> 5; matrix products, arithmetic and copies ran while one was open for 17% -> 28% of each run, Pallas kernels for 0% -> 0%
where the time goes in v1:
time: 194 us; the launch traced here: 193 us
  waiting for transfers between devices  84.8 us (44%)
  local copies, waits for them, and re-layouts  26.9 us (14%)
  matrix products  24.5 us (13%)
  other arithmetic  22 us (11%)
  starting transfers between devices  18.6 us (10%)
  between operations  16.1 us (8%)
    reduce_scatter x1, waiting for transfers between devices, on_device(): lax.psum_scatter(partial_grad, 'feat', scatter_dimension=1, tiled=True)  43.2 us
    ppermute x2, waiting for transfers between devices, collected_by_bits(): other = lax.ppermute(tiles, axis, [(i, i ^ apart) for i in range(devices)])  22.5 us
    ppermute x12, starting transfers between devices, shifted(): return lax.ppermute(block, axis, route)  12.8 us
    psum x1, waiting for transfers between devices, on_device(): grad_w = lax.psum(weight_term, 'blk')  11.9 us
    ppermute x12, waiting for transfers between devices, shifted(): return lax.ppermute(block, axis, route)  7.09 us
    dot_general x4, local copies, waits for them, and re-layouts, on_device(): jnp.einsum('sij,sjf->sif', tile_value[0, offset], arrived, preferred_elem...  6.15 us
    mul x4, other arithmetic, on_device(): slot_products(offset)  5.95 us
    gather x5, local copies, waits for them, and re-layouts, slot_products(): picked = jnp.take(grad_blocks, tile_row[0, offset], axis=0)  5.78 us
  transfers between devices with their start and end apart: 16, of which 5 were waited for; matrix products, arithmetic and copies ran while one was open for 28% of the time, Pallas kernels for 0%

profile of v1, /device:TPU:0, one launch (start us, length us, event | category | flops | bytes accessed | tf_op | source)
XLA Modules:
  0.0 192.8 jit_solution(5395370869966958696)
XLA Ops:
  8.1 3.1 %collective-permute-start = (bf16[1,1024,128]{2,1,0:T(8,128)(2,1)}, bf16[1,1024,128]{2,1,0:T(8,128)(2,1)S(1)}, u32[]{:S(2)}, u32[]{:S(2)}) collective-permute-start(bf16[1,1024,128]{2,1,0:T(8,128)(2,1)} %bitcast.180), channel_id=1, source_target_pairs={{0,1},{1,0},{2,3},{3,2},{4,5},{5,4},{6,7},{7,6},{8,9},{9,8},{10,11... | collective-permute-start | bytes 786440 | tf_op jit(solution)/shard_map/ppermute | solution.py:18
  11.9 2.4 %collective-permute-start.2 = (s32[8]{0:T(128)S(1)}, s32[8]{0:T(128)S(1)}, u32[]{:S(2)}, u32[]{:S(2)}) collective-permute-start(s32[8]{0:T(128)S(1)} %get-tuple-element.31), channel_id=1, source_target_pairs={{8,0},{12,4},{16,8},{20,12},{24,16},{28,20},{0,24},{4,28},{9,1},{1... | collective-permute-start | bytes 104 | tf_op jit(solution)/shard_map/ppermute | solution.py:32
  16.6 1.3 compare_and_fusion.2
  24.2 2.7 %collective-permute-start.1 = (bf16[2,1024,128]{2,1,0:T(8,128)(2,1)S(1)}, bf16[2,1024,128]{2,1,0:T(8,128)(2,1)S(1)}, u32[]{:S(2)}, u32[]{:S(2)}) collective-permute-start(bf16[2,1024,128]{2,1,0:T(8,128)(2,1)S(1)} %get-tuple-element.19), channel_id=1, source_target_pairs={{0,2},{1,3},{2,0},{3,1},{4,6},{5,7},{6,4},{7,5},{8,10},{9,11},{10,... | collective-permute-start | bytes 1572872 | tf_op jit(solution)/shard_map/ppermute | solution.py:18
  28.5 22.5 %collective-permute-done.1 = bf16[2,1024,128]{2,1,0:T(8,128)(2,1)S(1)} collective-permute-done((bf16[2,1024,128]{2,1,0:T(8,128)(2,1)S(1)}, bf16[2,1024,128]{2,1,0:T(8,128)(2,1)S(1)}, u32[]{:S(2)}, u32[]{:S(2)}) %collective-permute-start.1) | collective-permute-done | bytes 524320 | tf_op jit(solution)/shard_map/ppermute | solution.py:18
  58.4 1.4 broadcast_select_fusion.2
  60.6 1.4 broadcast_select_fusion.1
  62.0 2.6 %collective-permute-start.7 = (bf16[8,128,128]{2,1,0:T(8,128)(2,1)}, bf16[8,128,128]{2,1,0:T(8,128)(2,1)}, u32[]{:S(2)}, u32[]{:S(2)}) collective-permute-start(bf16[8,128,128]{2,1,0:T(8,128)(2,1)} %broadcast_select_fusion.1), channel_id=1, source_target_pairs={{4,0},{8,4},{12,8},{16,12},{20,16},{24,20},{28,24},{0,28},{5,1},{9... | collective-permute-start | bytes 786440 | tf_op jit(solution)/shard_map/ppermute | solution.py:32
  69.7 2.1 %fusion.23 = f32[8,128,128]{2,1,0:T(8,128)} fusion(bf16[8,128,128]{2,1,0:T(8,128)(2,1)} %collective-permute-done.5, bf16[1,5,8,128,128]{4,3,2,1,0:T(8,128)(2,1)S(1)} %copy-done.1), kind=kOutput, calls=%fused_computation.53 | convolution fusion | flops 33554432 | bytes 1048576 | tf_op jit(solution)/shard_map/sij,sjf->sif/dot_general | solution.py:68
  72.8 2.1 %copy.17 = f32[8,128,128]{1,0,2:T(8,128)} copy(f32[8,128,128]{2,1,0:T(8,128)} %fusion.23) | data formatting | bytes 1048576 | tf_op jit(solution)/shard_map/sij,sjf->sif/dot_general | solution.py:68
  78.3 2.0 %copy.19 = f32[8,128,128]{1,0,2:T(8,128)} copy(f32[8,128,128]{2,1,0:T(8,128)} %fusion.15) | data formatting | bytes 1048576 | tf_op jit(solution)/shard_map/sij,sjf->sif/dot_general | solution.py:68
  80.4 1.5 convolution_add_fusion.5
  87.1 1.9 %multiply_bitcast_fusion.3 = f32[8,128,128]{2,0,1:T(8,128)} fusion(f32[8,128,128]{1,0,2:T(8,128)} %copy.21, f32[8]{0:T(128)S(1)} %copy-done.11), kind=kLoop, calls=%fused_computation.37 | loop fusion | flops 131072 | bytes 1048608 | tf_op jit(solution)/shard_map/mul | solution.py:96
  89.0 1.9 collective-permute-start.10
  91.5 1.4 gather_fusion.8
  92.9 1.3 fusion.17
  95.2 1.9 %multiply_bitcast_fusion.1 = f32[8,128,128]{2,0,1:T(8,128)} fusion(f32[8,128,128]{1,0,2:T(8,128)} %copy.23, f32[8]{0:T(128)S(1)} %copy-done.10), kind=kLoop, calls=%fused_computation.35 | loop fusion | flops 131072 | bytes 1048608 | tf_op jit(solution)/shard_map/mul | solution.py:96
  97.2 1.5 gather_fusion.9
  101.0 2.0 %multiply_bitcast_fusion = f32[8,128,128]{2,0,1:T(8,128)} fusion(f32[8,128,128]{1,0,2:T(8,128)} %copy.24, f32[8]{0:T(128)S(1)} %copy-done.9), kind=kLoop, calls=%fused_computation.34 | loop fusion | flops 131072 | bytes 1048608 | tf_op jit(solution)/shard_map/mul | solution.py:96
  103.2 1.4 gather_fusion.7
  104.9 2.1 %fusion.21 = f32[8,128,128]{2,1,0:T(8,128)} fusion(bf16[8,128,128]{2,1,0:T(8,128)(2,1)} %gather_fusion.7, pred[8]{0:T(512)(128)(4,1)S(1)} %copy-done.12, bf16[1,5,8,128,128]{4,3,2,1,0:T(8,128)(2,1)S(1)} %copy-done.1), kind=kOutput, calls=%fused_computation.51 | convolution fusion | flops 33685504 | bytes 1049088 | tf_op jit(solution)/shard_map/sji,sjf->sif/dot_general | solution.py:83
  108.7 2.7 %collective-permute-start.11 = (f32[8,128,128]{2,0,1:T(8,128)S(1)}, f32[8,128,128]{2,0,1:T(8,128)S(1)}, u32[]{:S(2)}, u32[]{:S(2)}) collective-permute-start(f32[8,128,128]{2,0,1:T(8,128)S(1)} %multiply_bitcast_fusion.2), channel_id=1, source_target_pairs={{4,0},{8,4},{12,8},{16,12},{20,16},{24,20},{28,24},{0,28},{5,1},{9... | collective-permute-start | bytes 1572872 | tf_op jit(solution)/shard_map/ppermute | solution.py:32
  111.8 1.4 fusion.67
  113.3 5.7 %collective-permute-done.13 = f32[8,128,128]{2,0,1:T(8,128)} collective-permute-done((f32[8,128,128]{2,0,1:T(8,128)}, f32[8,128,128]{2,0,1:T(8,128)}, u32[]{:S(2)}, u32[]{:S(2)}) %collective-permute-start.13) | collective-permute-done | bytes 524320 | tf_op jit(solution)/shard_map/ppermute | solution.py:32
  119.0 1.4 fusion.70
  120.4 1.4 convolution_add_fusion.1
  121.8 1.3 collective-permute-done.11
  123.7 1.8 fusion.91
  126.8 43.2 %reduce-scatter.2.cloned.1.call-done = f32[1024,128]{1,0:T(8,128)} async-done(((f32[1024,512]{1,0:T(8,128)}), f32[1024,128]{1,0:T(8,128)}) %reduce-scatter.2.cloned.1.call-update) | async-done | bytes 524304 | tf_op jit(solution)/shard_map/reduce_scatter | solution.py:114
  169.9 1.8 convert_element_type.89
  171.7 11.9 %all-reduce.2.cloned.1.call-done = f32[512,128]{1,0:T(8,128)} async-done(((f32[512,128]{1,0:T(8,128)}), f32[512,128]{1,0:T(8,128)}) %all-reduce.2.cloned.1.call-update) | async-done | bytes 262160 | tf_op jit(solution)/shard_map/psum | solution.py:110
  183.6 1.7 copy.32
  (143 shorter events, 41.7 us)
Async XLA Ops:
  8.0 43.8 %copy-start = (bf16[512,128]{1,0:T(8,128)(2,1)S(1)}, bf16[512,128]{1,0:T(8,128)(2,1)}, u32[]{:S(2)}) copy-start(bf16[512,128]{1,0:T(8,128)(2,1)} %param.10) | copy-start | bytes 393220
  8.0 161.9 %reduce-scatter.2.cloned.1.call-start = ((), (), s32[]{:S(2)}) async-start(), calls=%async_computation.1 | async-start | bytes 2621440 | tf_op jit(solution)/shard_map/reduce_scatter | solution.py:114
  8.1 14.9 %collective-permute-start = (bf16[1,1024,128]{2,1,0:T(8,128)(2,1)}, bf16[1,1024,128]{2,1,0:T(8,128)(2,1)S(1)}, u32[]{:S(2)}, u32[]{:S(2)}) collective-permute-start(bf16[1,1024,128]{2,1,0:T(8,128)(2,1)} %bitcast.180), channel_id=1, source_target_pairs={{0,1},{1,0},{2,3},{3,2},{4,5},{5,4},{6,7},{7,6},{8,9},{9,8},{10,11... | collective-permute-start | bytes 786440 | tf_op jit(solution)/shard_map/ppermute | solution.py:18
  11.9 9.9 %collective-permute-start.2 = (s32[8]{0:T(128)S(1)}, s32[8]{0:T(128)S(1)}, u32[]{:S(2)}, u32[]{:S(2)}) collective-permute-start(s32[8]{0:T(128)S(1)} %get-tuple-element.31), channel_id=1, source_target_pairs={{8,0},{12,4},{16,8},{20,12},{24,16},{28,20},{0,24},{4,28},{9,1},{1... | collective-permute-start | bytes 104 | tf_op jit(solution)/shard_map/ppermute | solution.py:32
  14.3 7.4 %collective-permute-start.4 = (s32[8]{0:T(128)S(1)}, s32[8]{0:T(128)S(1)}, u32[]{:S(2)}, u32[]{:S(2)}) collective-permute-start(s32[8]{0:T(128)S(1)} %get-tuple-element.30), channel_id=1, source_target_pairs={{4,0},{8,4},{12,8},{16,12},{20,16},{24,20},{28,24},{0,28},{5,1},{9... | collective-permute-start | bytes 104 | tf_op jit(solution)/shard_map/ppermute | solution.py:32
  14.3 8.0 %collective-permute-start.6 = (s32[8]{0:T(128)S(1)}, s32[8]{0:T(128)S(1)}, u32[]{:S(2)}, u32[]{:S(2)}) collective-permute-start(s32[8]{0:T(128)S(1)} %get-tuple-element.29), channel_id=1, source_target_pairs={{28,0},{0,4},{4,8},{8,12},{12,16},{16,20},{20,24},{24,28},{29,1},{... | collective-permute-start | bytes 104 | tf_op jit(solution)/shard_map/ppermute | solution.py:32
  14.8 8.1 %collective-permute-start.8 = (s32[8]{0:T(128)S(1)}, s32[8]{0:T(128)S(1)}, u32[]{:S(2)}, u32[]{:S(2)}) collective-permute-start(s32[8]{0:T(128)S(1)} %get-tuple-element.28), channel_id=1, source_target_pairs={{24,0},{28,4},{0,8},{4,12},{8,16},{12,20},{16,24},{20,28},{25,1},{... | collective-permute-start | bytes 104 | tf_op jit(solution)/shard_map/ppermute | solution.py:32
  22.4 5.1 %copy-start.22 = (s32[8]{0:T(128)}, s32[8]{0:T(128)S(1)}, u32[]{:S(2)}) copy-start(s32[8]{0:T(128)S(1)} %collective-permute-done.6) | copy-start | bytes 100
  23.0 5.0 %copy-start.20 = (s32[8]{0:T(128)}, s32[8]{0:T(128)S(1)}, u32[]{:S(2)}) copy-start(s32[8]{0:T(128)S(1)} %collective-permute-done.8) | copy-start | bytes 100
  24.2 26.8 %collective-permute-start.1 = (bf16[2,1024,128]{2,1,0:T(8,128)(2,1)S(1)}, bf16[2,1024,128]{2,1,0:T(8,128)(2,1)S(1)}, u32[]{:S(2)}, u32[]{:S(2)}) collective-permute-start(bf16[2,1024,128]{2,1,0:T(8,128)(2,1)S(1)} %get-tuple-element.19), channel_id=1, source_target_pairs={{0,2},{1,3},{2,0},{3,1},{4,6},{5,7},{6,4},{7,5},{8,10},{9,11},{10,... | collective-permute-start | bytes 1572872 | tf_op jit(solution)/shard_map/ppermute | solution.py:18
  51.9 3.4 %copy-start.1 = (bf16[1,5,8,128,128]{4,3,2,1,0:T(8,128)(2,1)S(1)}, bf16[1,5,8,128,128]{4,3,2,1,0:T(8,128)(2,1)}, u32[]{:S(2)}) copy-start(bf16[1,5,8,128,128]{4,3,2,1,0:T(8,128)(2,1)} %param.11) | copy-start | bytes 3932164
  53.8 14.7 %collective-permute-start.3 = (bf16[8,128,128]{2,1,0:T(8,128)(2,1)}, bf16[8,128,128]{2,1,0:T(8,128)(2,1)}, u32[]{:S(2)}, u32[]{:S(2)}) collective-permute-start(bf16[8,128,128]{2,1,0:T(8,128)(2,1)} %broadcast_select_fusion.3), channel_id=1, source_target_pairs={{24,0},{28,4},{0,8},{4,12},{8,16},{12,20},{16,24},{20,28},{25,1},{... | collective-permute-start | bytes 786440 | tf_op jit(solution)/shard_map/ppermute | solution.py:32
  58.4 6.9 %copy-start.24 = (pred[8]{0:T(512)(128)(4,1)S(1)}, pred[8]{0:T(512)(128)(4,1)}, u32[]{:S(2)}) copy-start(pred[8]{0:T(512)(128)(4,1)} %compare_and_fusion.5) | copy-start | bytes 28
  59.8 9.9 %collective-permute-start.5 = (bf16[8,128,128]{2,1,0:T(8,128)(2,1)}, bf16[8,128,128]{2,1,0:T(8,128)(2,1)}, u32[]{:S(2)}, u32[]{:S(2)}) collective-permute-start(bf16[8,128,128]{2,1,0:T(8,128)(2,1)} %broadcast_select_fusion.2), channel_id=1, source_target_pairs={{28,0},{0,4},{4,8},{8,12},{12,16},{16,20},{20,24},{24,28},{29,1},{... | collective-permute-start | bytes 786440 | tf_op jit(solution)/shard_map/ppermute | solution.py:32
  62.0 12.9 %collective-permute-start.7 = (bf16[8,128,128]{2,1,0:T(8,128)(2,1)}, bf16[8,128,128]{2,1,0:T(8,128)(2,1)}, u32[]{:S(2)}, u32[]{:S(2)}) collective-permute-start(bf16[8,128,128]{2,1,0:T(8,128)(2,1)} %broadcast_select_fusion.1), channel_id=1, source_target_pairs={{4,0},{8,4},{12,8},{16,12},{20,16},{24,20},{28,24},{0,28},{5,1},{9... | collective-permute-start | bytes 786440 | tf_op jit(solution)/shard_map/ppermute | solution.py:32
  66.1 11.1 %collective-permute-start.9 = (bf16[8,128,128]{2,1,0:T(8,128)(2,1)}, bf16[8,128,128]{2,1,0:T(8,128)(2,1)S(1)}, u32[]{:S(2)}, u32[]{:S(2)}) collective-permute-start(bf16[8,128,128]{2,1,0:T(8,128)(2,1)} %broadcast_select_fusion), channel_id=1, source_target_pairs={{8,0},{12,4},{16,8},{20,12},{24,16},{28,20},{0,24},{4,28},{9,1},{1... | collective-permute-start | bytes 786440 | tf_op jit(solution)/shard_map/ppermute | solution.py:32
  87.1 5.8 %copy-start.15 = (pred[8]{0:T(512)(128)(4,1)S(1)}, pred[8]{0:T(512)(128)(4,1)}, u32[]{:S(2)}) copy-start(pred[8]{0:T(512)(128)(4,1)} %get-tuple-element.26) | copy-start | bytes 28
  89.0 31.4 %collective-permute-start.10 = (f32[8,128,128]{2,0,1:T(8,128)}, f32[8,128,128]{2,0,1:T(8,128)}, u32[]{:S(2)}, u32[]{:S(2)}) collective-permute-start(f32[8,128,128]{2,0,1:T(8,128)} %multiply_bitcast_fusion.3), channel_id=1, source_target_pairs={{8,0},{12,4},{16,8},{20,12},{24,16},{28,20},{0,24},{4,28},{9,1},{1... | collective-permute-start | bytes 1572872 | tf_op jit(solution)/shard_map/ppermute | solution.py:32
  91.5 3.7 %copy-start.10 = (f32[8]{0:T(128)S(1)}, f32[8]{0:T(128)}, u32[]{:S(2)}) copy-start(f32[8]{0:T(128)} %get-tuple-element.35) | copy-start | bytes 100
  94.2 4.5 %copy-start.14 = (pred[8]{0:T(512)(128)(4,1)S(1)}, pred[8]{0:T(512)(128)(4,1)}, u32[]{:S(2)}) copy-start(pred[8]{0:T(512)(128)(4,1)} %get-tuple-element.24) | copy-start | bytes 28
  97.1 14.7 %collective-permute-start.12 = (f32[8,128,128]{2,0,1:T(8,128)}, f32[8,128,128]{2,0,1:T(8,128)}, u32[]{:S(2)}, u32[]{:S(2)}) collective-permute-start(f32[8,128,128]{2,0,1:T(8,128)} %multiply_bitcast_fusion.1), channel_id=1, source_target_pairs={{28,0},{0,4},{4,8},{8,12},{12,16},{16,20},{20,24},{24,28},{29,1},{... | collective-permute-start | bytes 1572872 | tf_op jit(solution)/shard_map/ppermute | solution.py:32
  97.2 3.9 %copy-start.9 = (f32[8]{0:T(128)S(1)}, f32[8]{0:T(128)}, u32[]{:S(2)}) copy-start(f32[8]{0:T(128)} %get-tuple-element.34) | copy-start | bytes 100
  100.0 4.6 %copy-start.13 = (pred[8]{0:T(512)(128)(4,1)S(1)}, pred[8]{0:T(512)(128)(4,1)}, u32[]{:S(2)}) copy-start(pred[8]{0:T(512)(128)(4,1)} %get-tuple-element.22) | copy-start | bytes 28
  101.0 3.9 %copy-start.12 = (pred[8]{0:T(512)(128)(4,1)S(1)}, pred[8]{0:T(512)(128)(4,1)}, u32[]{:S(2)}) copy-start(pred[8]{0:T(512)(128)(4,1)} %get-tuple-element.4) | copy-start | bytes 28
  103.0 16.0 %collective-permute-start.13 = (f32[8,128,128]{2,0,1:T(8,128)}, f32[8,128,128]{2,0,1:T(8,128)}, u32[]{:S(2)}, u32[]{:S(2)}) collective-permute-start(f32[8,128,128]{2,0,1:T(8,128)} %multiply_bitcast_fusion), channel_id=1, source_target_pairs={{24,0},{28,4},{0,8},{4,12},{8,16},{12,20},{16,24},{20,28},{25,1},{... | collective-permute-start | bytes 1572872 | tf_op jit(solution)/shard_map/ppermute | solution.py:32
  104.9 3.4 %copy-start.8 = (f32[8]{0:T(128)S(1)}, f32[8]{0:T(128)}, u32[]{:S(2)}) copy-start(f32[8]{0:T(128)} %get-tuple-element.32) | copy-start | bytes 100
  108.5 3.4 %copy-start.23 = (s32[8]{0:T(128)S(1)}, s32[8]{0:T(128)}, u32[]{:S(2)}) copy-start(s32[8]{0:T(128)} %copy-done.22) | copy-start | bytes 100
  108.7 10.3 %copy-start.21 = (s32[8]{0:T(128)S(1)}, s32[8]{0:T(128)}, u32[]{:S(2)}) copy-start(s32[8]{0:T(128)} %copy-done.20) | copy-start | bytes 100
  108.7 14.4 %collective-permute-start.11 = (f32[8,128,128]{2,0,1:T(8,128)S(1)}, f32[8,128,128]{2,0,1:T(8,128)S(1)}, u32[]{:S(2)}, u32[]{:S(2)}) collective-permute-start(f32[8,128,128]{2,0,1:T(8,128)S(1)} %multiply_bitcast_fusion.2), channel_id=1, source_target_pairs={{4,0},{8,4},{12,8},{16,12},{20,16},{24,20},{28,24},{0,28},{5,1},{9... | collective-permute-start | bytes 1572872 | tf_op jit(solution)/shard_map/ppermute | solution.py:32
  111.8 8.6 %copy-start.19 = (s32[8]{0:T(128)S(1)}, s32[8]{0:T(128)}, u32[]{:S(2)}) copy-start(s32[8]{0:T(128)} %copy-done.18) | copy-start | bytes 100
  113.2 9.9 %copy-start.26 = (s32[8]{0:T(128)S(1)}, s32[8]{0:T(128)}, u32[]{:S(2)}) copy-start(s32[8]{0:T(128)} %copy-done.25) | copy-start | bytes 100
  125.5 58.1 %all-reduce.2.cloned.1.call-start = ((), (), s32[]{:S(2)}) async-start(), calls=%async_computation.2 | async-start | bytes 524288 | tf_op jit(solution)/shard_map/psum | solution.py:110
  (11 other events, 21.3 us)
Sparse Core Ops, SparseCore 0:
  125.7 44.2 reduce-scatter.1
Sparse Core Ops, SparseCore 1:
  129.6 54.0 all-reduce.1
